TPU v7x, 32 devices: a whole 2x2x4 slice. The times are simulated.
32 devices in a mesh: row: 4 (over y, x), col: 8 (over z, core).
Axes of the slice: x: 2, y: 2, z: 4, core: 2. Of those that a mesh axis runs over, the one named last changes fastest.
Arguments:
- amplitudes: bfloat16 [4096, 16384], P('col', 'row'), may hold values from -6 to 6
- integrals: bfloat16 [4096, 16384], P('row', 'col'), may hold values from -0.09375 to 0.09375
- tile_mask: int32 [64, 256], P(None, 'row'), may hold values from 0 to 1, as said below
- occ_energy: float32 [4], replicated, may hold values from -1 to -0.2
- virt_energy: float32 [4096], replicated, may hold values from 0.2 to 1.5
Outputs:
- update: bfloat16 [16384, 16384], P(('row', 'col'))
Inputs may be any that keep to these rules, and one draw needn't show every extreme that they name: `tile_mask`: 0 drops a tile, 1 keeps it; the share of kept tiles differs strongly between groups of (ia) rows.
All inputs are finite; a program needn't handle non-finite values.
Results may differ from a plain program's by a relative error of at most 0.0049.
Values may be sent and summed in bfloat16 or wider, within the bound.
A program may use at most 192 MiB of HBM per device.

v0:
```python
import jax
import jax.numpy as jnp
from jax import lax
from jax.sharding import PartitionSpec as P

TILE = 64


def local(amplitudes, integrals, tile_mask, occ_energy, virt_energy):
    col_count = lax.axis_size("col")
    row_place = lax.axis_index("row")
    col_place = lax.axis_index("col")
    local_depth, local_width = amplitudes.shape
    tile_rows = local_depth // TILE
    tile_cols = local_width // TILE
    own_mask = lax.dynamic_slice_in_dim(tile_mask, col_place * tile_rows, tile_rows, 0)
    keep_tiles = own_mask.astype(jnp.bfloat16)
    masked = (
        amplitudes.reshape(tile_rows, TILE, tile_cols, TILE) * keep_tiles[:, None, :, None]
    ).reshape(local_depth, local_width)
    whole_panel = lax.all_gather(integrals, "row", axis=0, tiled=True)
    left_rows = lax.all_gather(masked, "col", axis=0, tiled=True)
    product_block = lax.dot_general(
        left_rows, whole_panel, (((0,), (0,)), ((), ())), preferred_element_type=jnp.float32
    )
    cycle_block = product_block.astype(jnp.bfloat16)
    flat_rows = lax.all_to_all(cycle_block, "col", split_axis=0, concat_axis=1, tiled=True)
    rows_here, total_cols = flat_rows.shape
    pieces = total_cols // rows_here
    arrived = lax.all_to_all(
        flat_rows.reshape(rows_here, pieces, rows_here),
        ("row", "col"),
        split_axis=1,
        concat_axis=1,
        tiled=True,
    )
    mirrored = jnp.transpose(arrived, (2, 1, 0)).reshape(rows_here, total_cols)
    pair_gap = (virt_energy[None, :] - occ_energy[:, None]).reshape(total_cols)
    flat_place = row_place * col_count + col_place
    row_gap = lax.dynamic_slice_in_dim(pair_gap, flat_place * rows_here, rows_here, 0)
    summed = flat_rows.astype(jnp.float32) + mirrored.astype(jnp.float32)
    return (summed / (row_gap[:, None] + pair_gap[None, :])).astype(jnp.bfloat16)


def solution(mesh):
    return jax.shard_map(
        local,
        mesh=mesh,
        in_specs=(P("col", "row"), P("row", "col"), P(None, "row"), P(), P()),
        out_specs=P(("row", "col"), None),
        check_vma=False,
    )
```

profile of v0, /device:TPU:0, one launch (start us, length us, event | category | flops | bytes accessed | tf_op | source)
XLA Modules:
  0.0 1402.9 jit_solution(14816292952681816901)
XLA Ops:
  6.5 0.0 all-gather.5.cloned.1.call-start
  6.5 0.7 all-gather.5.cloned.1.call-update
  7.3 0.0 all-gather.3.cloned.1.call-start
  7.3 0.7 dynamic-slice_convert_fusion
  8.0 5.6 mul.21
  13.6 12.6 mul.22
  26.3 7.9 mul.23
  34.1 0.0 all-gather.3.cloned.1.call-update
  34.2 135.1 %all-gather.5.cloned.1.call-done = bf16[4096,2048]{1,0:T(8,128)(2,1)} async-done(((bf16[1024,2048]{1,0:T(8,128)(2,1)}), bf16[4096,2048]{1,0:T(8,128)(2,1)}) %all-gather.5.cloned.1.call-update) | async-done | bytes 16777232 | tf_op jit(solution)/shard_map/all_gather | solution.py:21
  169.2 290.2 %all-gather.3.cloned.1.call-done = bf16[4096,4096]{1,0:T(8,128)(2,1)} async-done(((bf16[512,4096]{1,0:T(8,128)(2,1)}), bf16[4096,4096]{1,0:T(8,128)(2,1)}) %all-gather.3.cloned.1.call-update) | async-done | bytes 33554448 | tf_op jit(solution)/shard_map/all_gather | solution.py:22
  459.4 79.4 %convolution_convert_fusion = bf16[4096,2048]{1,0:T(8,128)(2,1)} fusion(bf16[4096,4096]{1,0:T(8,128)(2,1)} %all-gather.3.cloned.1.call-done, bf16[4096,2048]{1,0:T(8,128)(2,1)} %all-gather.5.cloned.1.call-done), kind=kOutput, calls=%fused_computation.4 | convolution fusion | flops 68727865344 | bytes 67108864 | tf_op jit(solution)/shard_map/dot_general | solution.py:23
  538.9 21.6 %copy.9 = bf16[8,512,2048]{1,2,0:T(8,128)(2,1)} copy(bf16[8,512,2048]{2,1,0:T(8,128)(2,1)} %bitcast.20) | data formatting | bytes 33554432 | tf_op jit(solution)/shard_map/all_to_all | solution.py:27
  560.5 371.1 %all_to_all.21 = bf16[8,512,2048]{1,2,0:T(8,128)(2,1)} all-to-all(bf16[8,512,2048]{1,2,0:T(8,128)(2,1)} %copy.9), channel_id=1, replica_groups=mesh['row'=4,'col'=8] {'col'}, dimensions={0} | all-to-all | bytes 33554432 | tf_op jit(solution)/shard_map/all_to_all | solution.py:27
  931.6 0.0 copy-start
  931.6 0.0 copy-start.1
  931.6 4.0 all-to-all-start.1
  935.7 0.0 copy-done
  935.7 0.0 copy-done.1
  935.7 0.1 subtract_bitcast_fusion
  935.8 0.1 dynamic_slice.7
  935.9 364.4 %all-to-all-done.1 = bf16[512,32,512]{0,2,1:T(8,128)(2,1)} async-done(((bf16[512,32,512]{0,2,1:T(8,128)(2,1)}), bf16[512,32,512]{0,2,1:T(8,128)(2,1)}, u32[]{:S(2)}, u32[]{:S(2)}) %all-to-all-start.1) | async-done | bytes 16777248 | tf_op jit(solution)/shard_map/all_to_all | solution.py:30
  1300.2 18.8 %convert_bitcast_fusion = f32[512,32,512]{2,0,1:T(8,128)} fusion(bf16[512,32,512]{0,2,1:T(8,128)(2,1)} %all-to-all-done.1), kind=kLoop, calls=%fused_computation.3 | loop fusion | flops 8388608 | bytes 50331648 | tf_op jit(solution)/shard_map/convert_element_type | solution.py:41
  1319.0 33.4 %copy.10 = f32[512,32,512]{0,2,1:T(8,128)} copy(f32[512,32,512]{2,0,1:T(8,128)} %convert_bitcast_fusion) | data formatting | bytes 67108864 | tf_op jit(solution)/shard_map/convert_element_type | solution.py:41
  1352.4 22.5 %fusion.1 = bf16[512,16384]{0,1:T(8,128)(2,1)} fusion(f32[512,32,512]{0,2,1:T(8,128)} %copy.10, bf16[8,512,2048]{1,2,0:T(8,128)(2,1)} %all_to_all.21, f32[16384]{0:T(1024)S(1)} %bitcast.22, f32[512]{0:T(512)S(1)} %dynamic_slice.7), kind=kLoop, calls=%fused_computation.2 | loop fusion | flops 41943040 | bytes 67176448 | tf_op jit(solution)/shard_map/convert_element_type | solution.py:42
  1374.9 21.2 %copy.11 = bf16[512,16384]{1,0:T(8,128)(2,1)} copy(bf16[512,16384]{0,1:T(8,128)(2,1)} %fusion.1) | data formatting | bytes 33554432 | tf_op jit(solution)/shard_map/convert_element_type | solution.py:42
  (1 shorter events, 0.0 us)
Async XLA Ops:
  6.5 162.7 %all-gather.5.cloned.1.call-start = ((), (), s32[]{:S(2)}) async-start(), calls=%async_computation.3 | async-start | bytes 20971520 | tf_op jit(solution)/shard_map/all_gather | solution.py:21
  7.3 452.2 %all-gather.3.cloned.1.call-start = ((), (), s32[]{:S(2)}) async-start(), calls=%async_computation.2 | async-start | bytes 37748736 | tf_op jit(solution)/shard_map/all_gather | solution.py:22
  931.6 4.0 copy-start
  931.6 4.0 copy-start.1
  931.6 368.6 %all-to-all-start.1 = ((bf16[512,32,512]{0,2,1:T(8,128)(2,1)}), bf16[512,32,512]{0,2,1:T(8,128)(2,1)}, u32[]{:S(2)}, u32[]{:S(2)}) async-start(bf16[512,32,512]{0,2,1:T(8,128)(2,1)} %bitcast.19), calls=%async_computation.1 | async-start | bytes 33554432 | tf_op jit(solution)/shard_map/all_to_all | solution.py:30
Sparse Core Ops, SparseCore 0:
  9.2 160.0 all-gather.4
  170.8 288.5 all-gather.2
where the time goes:
time: 1410 us; the launch traced here: 1400 us
  waiting for transfers between devices  790 us (56%)
  blocking collectives  371 us (26%)
  local copies, waits for them, and re-layouts  94.5 us (7%)
  matrix products  79.4 us (6%)
  other arithmetic  50 us (4%)
    all_to_all x1, blocking collectives, local(): lax.all_to_all(cycle_block, 'col', split_axis=0, concat_axis=1, tiled=True)  371 us
    all_to_all x1, waiting for transfers between devices, local(): lax.all_to_all(flat_rows.reshape(rows_here, pieces, rows_here), ('row', '...  364 us
    all_gather x1, waiting for transfers between devices, local(): left_rows = lax.all_gather(masked, 'col', axis=0, tiled=True)  290 us
    all_gather x1, waiting for transfers between devices, local(): whole_panel = lax.all_gather(integrals, 'row', axis=0, tiled=True)  135 us
    dot_general x1, matrix products, local(): lax.dot_general(left_rows, whole_panel, (((0,), (0,)), ((), ())), preferr...  79.4 us
    convert_element_type x1, local copies, waits for them, and re-layouts, local(): summed = flat_rows.astype(jnp.float32) + mirrored.astype(jnp.float32)  33.4 us
  transfers between devices with their start and end apart: 3, of which 3 were waited for; matrix products, arithmetic and copies ran while one was open for 2% of the time, Pallas kernels for 0%

commit v1 on v0

v1 whole, which is shorter than its diff:
```python
import functools

import jax
import jax.numpy as jnp
from jax import lax
from jax.experimental import pallas as pl
from jax.experimental.pallas import tpu as pltpu
from jax.sharding import PartitionSpec as P

TILE = 64
PIECES = 2
MESH = pl.DeviceIdType.MESH


def gather_kernel(
    n_row, n_col, a_ref, i_ref, a_full, a_r, i_q, i_r, i_g,
    send_sem, local_sem, sem_a, sem_g, sem_q, sem_ar, sem_ir,
):
    r = lax.axis_index("row")
    c = lax.axis_index("col")
    chips = n_col // 2
    k = c // 2
    p = c % 2
    partner = c + 1 - 2 * p
    d = a_ref.shape[0] // PIECES
    e = i_ref.shape[0] // PIECES
    j = i_ref.shape[1]
    q = a_ref.shape[1] // n_col
    side = c // chips

    barrier = pltpu.get_barrier_semaphore()

    def greet(row, col):
        pl.semaphore_signal(barrier, inc=1, device_id=(row, col), device_id_type=MESH)

    greet(r, partner)
    count = 1 + 2 * (n_row - 1)
    for m in range(1, n_row):
        greet((r + m) % n_row, c)
        greet((r + m) % n_row, partner)

    greet(r, (c + 2) % n_col)
    greet(r, (c - 2 + n_col) % n_col)
    pl.semaphore_wait(barrier, count + 2)

    pending = []
    counts = [0, 0]

    def run(cond, body):
        if cond is None:
            body()
        else:
            pl.when(cond)(body)

    def send(src, dst, recv, row, col, cond=None):
        sem = send_sem.at[counts[0]]
        counts[0] += 1
        copy = pltpu.make_async_remote_copy(
            src_ref=src, dst_ref=dst, send_sem=sem, recv_sem=recv,
            device_id=(row, col), device_id_type=MESH,
        )
        run(cond, copy.start)
        pending.append((cond, copy.wait_send))

    def local(src, dst, cond=None):
        sem = local_sem.at[counts[1]]
        counts[1] += 1
        copy = pltpu.make_async_copy(src, dst, sem)
        run(cond, copy.start)
        pending.append((cond, copy.wait))

    def arrived(ref, sem, cond=None):
        run(cond, pltpu.make_async_copy(ref, ref, sem).wait)

    def both(x, y):
        return y if x is None else (x if y is None else jnp.logical_and(x, y))

    def a_rows(block, h):
        return pl.ds(pl.multiple_of((block * PIECES + h) * d, d), d)

    def i_rows(row, h):
        return pl.ds(pl.multiple_of((row * PIECES + h) * e, e), e)

    def i_cols(parity):
        return pl.ds(pl.multiple_of(parity * j, j), j)

    own = pl.ds(pl.multiple_of(c * q, q), q)

    def a_to_rows(src, block, h, cond=None):
        rows = a_rows(block, h)
        for m in range(1, n_row):
            send(src.at[:, own], a_r.at[m - 1, rows, :], sem_ar, (r + m) % n_row, c, cond)

    def i_out(src, block, h, cond=None):
        rows = i_rows(r, h)
        elsewhere = both(cond, block != r)
        send(src, i_q.at[rows, i_cols(p)], sem_q.at[r, p, h], block, c, elsewhere)
        here = both(cond, block == r)
        local(src, i_q.at[rows, i_cols(p)], here)
        send(src, i_q.at[rows, i_cols(p)], sem_q.at[r, p, h], r, partner, here)
        holder = both(cond, side == p)
        for t in range(2):
            col = 2 * k + t
            part = src.at[:, pl.ds(pl.multiple_of((col - side * chips) * q, q), q)]
            for m in range(1, n_row):
                row = (r + m) % n_row
                slot = (row - block + n_row) % n_row
                send(part, i_r.at[slot, rows, :], sem_ir.at[r, h], row, col, holder)
            slot = (r - block + n_row) % n_row
            send(part, i_r.at[slot, rows, :], sem_ir.at[r, h], r, partner, both(holder, p != t))
            local(part, i_r.at[slot, rows, :], both(holder, p == t))

    up, down = k < chips - 1, k > 0
    for h in range(PIECES):
        a_own = a_ref.at[pl.ds(h * d, d), :]
        i_own = i_ref.at[pl.ds(h * e, e), :]
        dst_a = a_full.at[a_rows(c, h), :]
        for cond, col in ((up, c + 2), (down, c - 2)):
            send(i_own, i_g.at[k, pl.ds(h * e, e), :], sem_g.at[k, h], r, col, cond)
            send(a_own, dst_a, sem_a.at[c, h], r, col, cond)
        i_out(i_own, k, h)
        send(a_own, dst_a, sem_a.at[c, h], r, partner)
        a_to_rows(a_own, c, h)
        local(a_own, dst_a)

    def hand_q(h, cond):
        for m in range(1, n_row):
            row = (r + m) % n_row
            piece = i_q.at[i_rows(row, h), i_cols(p)]
            arrived(piece, sem_q.at[row, p, h], cond)
            send(piece, piece, sem_q.at[row, p, h], r, partner, cond)

    for s in range(1, chips):
        for h in range(PIECES):
            for sign in (-1, 1):
                far = k + sign * s
                there = far >= 0 if sign < 0 else far < chips
                onward = both(there, up if sign < 0 else down)
                g = i_g.at[jnp.clip(far, 0, chips - 1), pl.ds(h * e, e), :]
                col = c - 2 * sign
                block = 2 * far + p
                full = a_full.at[a_rows(jnp.clip(block, 0, n_col - 1), h), :]
                got_g = sem_g.at[jnp.clip(far, 0, chips - 1), h]
                got_a = sem_a.at[jnp.clip(block, 0, n_col - 1), h]
                arrived(g, got_g, there)
                send(g, g, got_g, r, col, onward)
                i_out(g, jnp.clip(far, 0, chips - 1), h, there)
                arrived(full, got_a, there)
                send(full, full, got_a, r, col, onward)
                send(full, full, got_a, r, partner, there)
                a_to_rows(full, jnp.clip(block, 0, n_col - 1), h, there)
            for sign in (-1, 1):
                far = k + sign * (s - 1)
                if s == 1 and sign > 0:
                    continue
                there = far >= 0 if sign < 0 else far < chips
                other = jnp.clip(2 * far + 1 - p, 0, n_col - 1)
                full = a_full.at[a_rows(other, h), :]
                arrived(full, sem_a.at[other, h], there)
                a_to_rows(full, other, h, there)
            hand_q(h, jnp.logical_or(r - k == s - 1, k - r == s - 1))
    for h in range(PIECES):
        for sign in (-1, 1):
            far = k + sign * (chips - 1)
            there = far >= 0 if sign < 0 else far < chips
            other = jnp.clip(2 * far + 1 - p, 0, n_col - 1)
            full = a_full.at[a_rows(other, h), :]
            arrived(full, sem_a.at[other, h], there)
            a_to_rows(full, other, h, there)
        hand_q(h, jnp.logical_or(r - k == chips - 1, k - r == chips - 1))

    for h in range(PIECES):
        for m in range(n_row):
            row = (r + m) % n_row
            arrived(i_q.at[i_rows(row, h), i_cols(1 - p)], sem_q.at[row, 1 - p, h])
            if m:
                arrived(i_r.at[:, i_rows(row, h), :], sem_ir.at[row, h])
        arrived(i_r.at[:, i_rows(r, h), :], sem_ir.at[r, h], side != p)
    arrived(a_r, sem_ar)
    for cond, wait in pending:
        run(cond, wait)


def sem_counts(n_row, n_col):
    chips = n_col // 2
    i_out = 2 + 2 * n_row
    sends = PIECES * (5 + i_out + n_row - 1)
    steps = chips - 1
    sends += PIECES * 2 * steps * (3 + i_out + n_row - 1)
    sends += PIECES * ((2 * steps - 1) * (n_row - 1) + steps * (n_row - 1))
    sends += PIECES * 3 * (n_row - 1)
    locals_ = PIECES * (4 + 2 * steps * 3)
    return sends, locals_


def gather(n_row, n_col, a, i):
    d, w = a.shape
    e, j = i.shape
    q = w // n_col
    depth = d * n_col
    chips = n_col // 2
    sends, locals_ = sem_counts(n_row, n_col)
    dma = pltpu.SemaphoreType.DMA
    hbm = pl.BlockSpec(memory_space=pl.ANY)
    shapes = [(depth, w), (n_row - 1, depth, q), (depth, w), (n_row, depth, q), (chips, e, j)]
    return pl.pallas_call(
        functools.partial(gather_kernel, n_row, n_col),
        out_shape=[jax.ShapeDtypeStruct(s, a.dtype) for s in shapes],
        in_specs=[hbm] * 2,
        out_specs=[hbm] * 5,
        scratch_shapes=[
            dma((sends,)), dma((locals_,)), dma((n_col, PIECES)), dma((chips, PIECES)),
            dma((n_row, 2, PIECES)), dma, dma((n_row, PIECES)),
        ],
        compiler_params=pltpu.CompilerParams(collective_id=0, has_side_effects=True),
    )(a, i)


def local(amplitudes, integrals, tile_mask, occ_energy, virt_energy):
    n_row = lax.axis_size("row")
    n_col = lax.axis_size("col")
    r = lax.axis_index("row")
    c = lax.axis_index("col")
    local_depth, local_width = amplitudes.shape
    tile_rows = local_depth // TILE
    tile_cols = local_width // TILE
    own_mask = lax.dynamic_slice_in_dim(tile_mask, c * tile_rows, tile_rows, 0)
    keep_tiles = own_mask.astype(jnp.bfloat16)
    masked = (
        amplitudes.reshape(tile_rows, TILE, tile_cols, TILE) * keep_tiles[:, None, :, None]
    ).reshape(local_depth, local_width)
    a_full, a_r, i_q, i_r, _ = gather(n_row, n_col, masked, integrals)
    q = local_width // n_col
    pair_gap = (virt_energy[None, :] - occ_energy[:, None]).reshape(-1)
    col_gap = lax.dynamic_slice_in_dim(pair_gap, r * local_width, local_width, 0)
    out = jnp.zeros((q, pair_gap.shape[0]), jnp.bfloat16)
    dims = (((0,), (0,)), ((), ()))
    landed = []
    for m in [*range(1, n_row), 0]:
        target = (r - m) % n_row
        left = a_r[m - 1] if m else lax.dynamic_slice_in_dim(a_full, c * q, q, 1)
        first = lax.dot_general(left, i_q, dims, preferred_element_type=jnp.float32)
        second = lax.dot_general(i_r[m], a_full, dims, preferred_element_type=jnp.float32)
        row_gap = lax.dynamic_slice_in_dim(pair_gap, target * local_width + c * q, q, 0)
        block = ((first + second) / (row_gap[:, None] + col_gap[None, :])).astype(jnp.bfloat16)
        if m:
            block = lax.ppermute(block, "row", [(s, (s - m) % n_row) for s in range(n_row)])
        landed.append((m, block))
    for m, block in landed:
        out = lax.dynamic_update_slice_in_dim(out, block, ((r + m) % n_row) * local_width, 1)
    return out


def solution(mesh):
    return jax.shard_map(
        local,
        mesh=mesh,
        in_specs=(P("col", "row"), P("row", "col"), P(None, "row"), P(), P()),
        out_specs=P(("row", "col"), None),
        check_vma=False,
    )
```

time: 1410 us -> 1040 us (0.74)
  waiting for transfers between devices: 790 us -> 90.2 us
  Pallas kernels: 0 us -> 636 us
  blocking collectives: 371 us -> 0 us
  matrix products: 79.4 us -> 192 us
  starting transfers between devices: 4.06 us -> 74.5 us
  local copies, waits for them, and re-layouts: 94.5 us -> 33.3 us
  other arithmetic: 50 us -> 8.76 us
    pallas_call x0 -> x1, Pallas kernels: none -> 636 us  [gather(): pl.pallas_call(functools.partial(gather_kernel, n_row, n_col), out_shape=...]
    all_gather x2 -> x0, waiting for transfers between devices: 425 us -> none  [the longest x1 290 us: local(): left_rows = lax.all_gather(masked, 'col', axis=0, tiled=True)]
    all_to_all x1 -> x0, blocking collectives: 371 us -> none  [local(): lax.all_to_all(cycle_block, 'col', split_axis=0, concat_axis=1, tiled=True)]
    all_to_all x1 -> x0, waiting for transfers between devices: 364 us -> none  [local(): lax.all_to_all(flat_rows.reshape(rows_here, pieces, rows_here), ('row', '...]
    dot_general x1 -> x8, matrix products: 79.4 us -> 192 us  [the longest x4 96.4 us: local(): first = lax.dot_general(left, i_q, dims, preferred_element_type=jnp.float32)]
    ppermute x0 -> x3, waiting for transfers between devices: none -> 90.2 us  [local(): lax.ppermute(block, 'row', [(s, (s - m) % n_row) for s in range(n_row)])]
    ppermute x0 -> x3, starting transfers between devices: none -> 74.5 us  [local(): lax.ppermute(block, 'row', [(s, (s - m) % n_row) for s in range(n_row)])]
    convert_element_type x2 -> x0, local copies, waits for them, and re-layouts: 54.5 us -> none  [the longest x1 33.4 us: local(): summed = flat_rows.astype(jnp.float32) + mirrored.astype(jnp.float32)]
  transfers between devices with their start and end apart: 3 -> 3, of which waited for: 3 -> 2; matrix products, arithmetic and copies ran while one was open for 2% -> 12% of each run, Pallas kernels for 0% -> 0%
where the time goes in v1:
time: 1040 us
  Pallas kernels  636 us (61%)
  matrix products  192 us (18%)
  waiting for transfers between devices  90.2 us (9%)
  starting transfers between devices  74.5 us (7%)
  local copies, waits for them, and re-layouts  33.3 us (3%)
    pallas_call x1, Pallas kernels, gather(): pl.pallas_call(functools.partial(gather_kernel, n_row, n_col), out_shape=...  636 us
    dot_general x4, matrix products, local(): first = lax.dot_general(left, i_q, dims, preferred_element_type=jnp.float32)  96.4 us
    dot_general x4, matrix products, local(): lax.dot_general(i_r[m], a_full, dims, preferred_element_type=jnp.float32)  96 us
    ppermute x3, waiting for transfers between devices, local(): lax.ppermute(block, 'row', [(s, (s - m) % n_row) for s in range(n_row)])  90.2 us
    ppermute x3, starting transfers between devices, local(): lax.ppermute(block, 'row', [(s, (s - m) % n_row) for s in range(n_row)])  74.5 us
  transfers between devices with their start and end apart: 3, of which 2 were waited for; matrix products, arithmetic and copies ran while one was open for 12% of the time, Pallas kernels for 0%

profile of v1, /device:TPU:0, one launch (start us, length us, event | category | flops | bytes accessed | tf_op | source)
XLA Modules:
  0.0 1035.7 jit_solution(12545843625685078264)
XLA Ops:
  0.0 0.8 subtract_bitcast_fusion
  0.8 0.7 dynamic-slice_convert_fusion
  1.5 5.6 mul.47
  7.1 12.0 %mul.48 = bf16[512,4096]{1,0:T(8,128)(2,1)} reshape(bf16[8,64,64,64]{3,2,1,0:T(8,128)(2,1)} %mul.47) | data formatting | bytes 8388608 | tf_op jit(solution)/shard_map/mul | solution.py:230
  19.2 7.2 mul.49.a_ref
  26.4 636.4 %shard_map.55 = (bf16[4096,4096]{1,0:T(8,128)(2,1)}, bf16[3,4096,512]{2,1,0:T(8,128)(2,1)}, bf16[4096,4096]{1,0:T(8,128)(2,1)}, bf16[4,4096,512]{2,1,0:T(8,128)(2,1)}, bf16[4,1024,2048]{2,1,0:T(8,128)(2,1)}) custom-call(bf16[512,4096]{1,0:T(8,128)(2,1)} %mul.49.a_ref, bf16[1024,2048]{1,0:T(8,128)(2,1)} %i_ref.1), custom_call_target="tpu_custom_call" | custom-call | tf_op jit(solution)/shard_map/pallas_call | solution.py:206
  662.8 0.0 copy-start.1
  662.8 24.5 %fusion.6 = f32[512,4096]{1,0:T(8,128)} fusion(bf16[4096,4096]{1,0:T(8,128)(2,1)} %get-tuple-element.10, bf16[3,4096,512]{2,1,0:T(8,128)(2,1)} %get-tuple-element.9), kind=kOutput, calls=%fused_computation.10 | convolution fusion | flops 17179869184 | bytes 46137344 | tf_op jit(solution)/shard_map/dot_general | solution.py:242
  687.3 0.1 fusion.21
  687.4 0.0 copy-done.1
  687.4 24.0 %divide_convert_fusion.2 = bf16[512,4096]{1,0:T(8,128)(2,1)} fusion(f32[512,4096]{1,0:T(8,128)} %fusion.6, bf16[4096,4096]{1,0:T(8,128)(2,1)} %get-tuple-element.12, f32[512]{0:T(512)S(1)} %get-tuple-element.15, bf16[4,4096,512]{2,1,0:T(8,128)(2,1)S(1)} %copy-done.1, f32[4096]{0:T(1024)S(1)} %dynamic_slice.23), kind=kOutput, calls=%fused_computation.2 | convolution fusion | flops 17188257792 | bytes 50350080 | tf_op jit(solution)/shard_map/dot_general | solution.py:243
  711.3 3.0 collective-permute-start.1
  714.4 24.0 %fusion.9 = f32[512,4096]{1,0:T(8,128)} fusion(bf16[4096,4096]{1,0:T(8,128)(2,1)} %get-tuple-element.10, bf16[3,4096,512]{2,1,0:T(8,128)(2,1)} %get-tuple-element.9), kind=kOutput, calls=%fused_computation.13 | convolution fusion | flops 17179869184 | bytes 46137344 | tf_op jit(solution)/shard_map/dot_general | solution.py:242
  738.4 23.9 %divide_convert_fusion.3 = bf16[512,4096]{1,0:T(8,128)(2,1)} fusion(f32[512,4096]{1,0:T(8,128)} %fusion.9, bf16[4096,4096]{1,0:T(8,128)(2,1)} %get-tuple-element.12, f32[4096]{0:T(1024)S(1)} %dynamic_slice.23, f32[512]{0:T(512)S(1)} %get-tuple-element.16, bf16[4,4096,512]{2,1,0:T(8,128)(2,1)S(1)} %copy-done.1), kind=kOutput, calls=%fused_computation.3 | convolution fusion | flops 17188257792 | bytes 50350080 | tf_op jit(solution)/shard_map/dot_general | solution.py:243
  762.2 70.7 %collective-permute-start = (bf16[512,4096]{1,0:T(8,128)(2,1)}, bf16[512,4096]{1,0:T(8,128)(2,1)}, u32[]{:S(2)}, u32[]{:S(2)}) collective-permute-start(bf16[512,4096]{1,0:T(8,128)(2,1)} %divide_convert_fusion.3), channel_id=1, source_target_pairs={{0,24},{8,0},{16,8},{24,16},{1,25},{9,1},{17,9},{25,17},{2,26},{10... | collective-permute-start | bytes 12582920 | tf_op jit(solution)/shard_map/ppermute | solution.py:247
  832.9 24.0 %fusion.3 = f32[512,4096]{1,0:T(8,128)} fusion(bf16[4096,4096]{1,0:T(8,128)(2,1)} %get-tuple-element.10, bf16[3,4096,512]{2,1,0:T(8,128)(2,1)} %get-tuple-element.9), kind=kOutput, calls=%fused_computation.7 | convolution fusion | flops 17179869184 | bytes 46137344 | tf_op jit(solution)/shard_map/dot_general | solution.py:242
  856.9 23.8 %divide_convert_fusion.1 = bf16[512,4096]{1,0:T(8,128)(2,1)} fusion(f32[512,4096]{1,0:T(8,128)} %fusion.3, bf16[4096,4096]{1,0:T(8,128)(2,1)} %get-tuple-element.12, f32[512]{0:T(512)S(1)} %get-tuple-element.14, bf16[4,4096,512]{2,1,0:T(8,128)(2,1)S(1)} %copy-done.1, f32[4096]{0:T(1024)S(1)} %dynamic_slice.23), kind=kOutput, calls=%fused_computation.1 | convolution fusion | flops 17188257792 | bytes 50350080 | tf_op jit(solution)/shard_map/dot_general | solution.py:243
  880.7 0.8 collective-permute-start.2
  881.5 24.0 %fusion.12 = f32[512,4096]{1,0:T(8,128)} fusion(bf16[4096,4096]{1,0:T(8,128)(2,1)} %get-tuple-element.10, bf16[4096,4096]{1,0:T(8,128)(2,1)} %get-tuple-element.12, s32[]{:T(128)S(6)} %select_n.80), kind=kOutput, calls=%fused_computation.16 | convolution fusion | flops 17179869184 | bytes 46137348 | tf_op jit(solution)/shard_map/dot_general | solution.py:242
  905.5 19.7 %collective-permute-done = bf16[512,4096]{1,0:T(8,128)(2,1)} collective-permute-done((bf16[512,4096]{1,0:T(8,128)(2,1)}, bf16[512,4096]{1,0:T(8,128)(2,1)}, u32[]{:S(2)}, u32[]{:S(2)}) %collective-permute-start) | collective-permute-done | bytes 4194336 | tf_op jit(solution)/shard_map/ppermute | solution.py:247
  925.2 1.2 broadcast_in_dim.2
  926.4 2.8 constant_dynamic-update-slice_fusion.2
  929.2 0.0 collective-permute-done.1
  929.2 2.8 constant_dynamic-update-slice_fusion.1
  931.9 70.5 %collective-permute-done.2 = bf16[512,4096]{1,0:T(8,128)(2,1)} collective-permute-done((bf16[512,4096]{1,0:T(8,128)(2,1)}, bf16[512,4096]{1,0:T(8,128)(2,1)}, u32[]{:S(2)}, u32[]{:S(2)}) %collective-permute-start.2) | collective-permute-done | bytes 4194336 | tf_op jit(solution)/shard_map/ppermute | solution.py:247
  1002.4 2.7 constant_dynamic-update-slice_fusion
  1005.2 0.0 copy-start
  1005.2 6.2 copy-done
  1011.4 24.3 %fusion = bf16[512,16384]{1,0:T(8,128)(2,1)} fusion(bf16[512,16384]{1,0:T(8,128)(2,1)} %copy-done, s32[]{:T(128)S(6)} %select_n.83, f32[512,4096]{1,0:T(8,128)} %fusion.12, bf16[4096,4096]{1,0:T(8,128)(2,1)} %get-tuple-element.12, f32[512]{0:T(512)S(1)} %get-tuple-element.13, bf16[4,4096,512]{2,1,0:T(8,128)(2,1)} %get-tuple-element.11, ...), kind=kOutput, calls=%fused_computation.4 | convolution fusion | flops 17188257792 | bytes 50350084 | tf_op jit(solution)/shard_map/dot_general | solution.py:243
  (2 shorter events, 0.0 us)
Async XLA Ops:
  662.8 24.6 %copy-start.1 = (bf16[4,4096,512]{2,1,0:T(8,128)(2,1)S(1)}, bf16[4,4096,512]{2,1,0:T(8,128)(2,1)}, u32[]{:S(2)}) copy-start(bf16[4,4096,512]{2,1,0:T(8,128)(2,1)} %get-tuple-element.11) | copy-start | bytes 50331652
  711.3 217.8 %collective-permute-start.1 = (bf16[512,4096]{1,0:T(8,128)(2,1)}, bf16[512,4096]{1,0:T(8,128)(2,1)}, u32[]{:S(2)}, u32[]{:S(2)}) collective-permute-start(bf16[512,4096]{1,0:T(8,128)(2,1)} %divide_convert_fusion.2), channel_id=1, source_target_pairs={{0,16},{8,24},{16,0},{24,8},{1,17},{9,25},{17,1},{25,9},{2,18},{10... | collective-permute-start | bytes 12582920 | tf_op jit(solution)/shard_map/ppermute | solution.py:247
  762.2 163.0 %collective-permute-start = (bf16[512,4096]{1,0:T(8,128)(2,1)}, bf16[512,4096]{1,0:T(8,128)(2,1)}, u32[]{:S(2)}, u32[]{:S(2)}) collective-permute-start(bf16[512,4096]{1,0:T(8,128)(2,1)} %divide_convert_fusion.3), channel_id=1, source_target_pairs={{0,24},{8,0},{16,8},{24,16},{1,25},{9,1},{17,9},{25,17},{2,26},{10... | collective-permute-start | bytes 12582920 | tf_op jit(solution)/shard_map/ppermute | solution.py:247
  880.7 121.7 %collective-permute-start.2 = (bf16[512,4096]{1,0:T(8,128)(2,1)}, bf16[512,4096]{1,0:T(8,128)(2,1)}, u32[]{:S(2)}, u32[]{:S(2)}) collective-permute-start(bf16[512,4096]{1,0:T(8,128)(2,1)} %divide_convert_fusion.1), channel_id=1, source_target_pairs={{0,8},{8,16},{16,24},{24,0},{1,9},{9,17},{17,25},{25,1},{2,10},{10... | collective-permute-start | bytes 12582920 | tf_op jit(solution)/shard_map/ppermute | solution.py:247
  1005.2 6.2 copy-start
